TPU v7x, 256 devices: a whole 4x4x8 slice. The times are simulated.
256 devices in a mesh: hid: 4 (over x_lo, core), tok: 64 (over x_hi, y, z).
Axes of the slice: x: 4 (x_hi: 2, x_lo: 2; x = x_hi * 2 + x_lo), y: 4, z: 8, core: 2. Of those that a mesh axis runs over, the one named last changes fastest.
Arguments:
- val_inputs: bfloat16 [256, 4096], P(None, 'tok'), may hold values from -6 to 6
- val_out_grad: bfloat16 [256, 4096], P(None, 'tok'), may hold values from -6 to 6
- w_gate: bfloat16 [4096, 14336], P('tok', 'hid'), may hold values from -0.09375 to 0.09375
- w_up: bfloat16 [4096, 14336], P('tok', 'hid'), may hold values from -0.09375 to 0.09375
- w_down: bfloat16 [14336, 4096], P('hid', 'tok'), may hold values from -0.046875 to 0.046875
- val_attn_inputs: bfloat16 [256, 4096], P('hid', 'tok'), may hold values from -6 to 6
- train_inputs: bfloat16 [163840, 4096], P(('hid', 'tok')), may hold values from -6 to 6
- train_grads: bfloat16 [163840, 4096], P(('hid', 'tok')), may hold values from -6 to 6
Outputs:
- influence: float32 [163840], P(('hid', 'tok'))
- val_grad: bfloat16 [256, 4096], P('hid', 'tok')
All inputs are finite; a program needn't handle non-finite values.
Results may differ from a plain program's by a relative error of at most 0.0036.
Values may be sent and summed in bfloat16 or wider, within the bound.
No kernel may reach another device: no remote copies, remote signals or barrier semaphores. Data moves between devices by JAX's collectives and lax.ppermute only.
A program may use at most 128 MiB of HBM per device.

v0:
```python
import math
import jax
import jax.numpy as jnp
from jax import lax
from jax.sharding import PartitionSpec as P


def dot_rows(left, right):
    return lax.dot_general(
        left, right, (((1,), (1,)), ((), ())), preferred_element_type=jnp.float32
    )


def act_grads(gate_pre, up_pre, hid_grad):
    logistic = jax.nn.sigmoid(gate_pre)
    grad_gate = (hid_grad * up_pre * logistic * (1.0 + gate_pre * (1.0 - logistic))).astype(
        jnp.bfloat16
    )
    grad_up = (hid_grad * gate_pre * logistic).astype(jnp.bfloat16)
    return (grad_gate, grad_up)


def pair_terms(train_in, train_gr, val_in, val_gr):
    in_gram = dot_rows(train_in, val_in)
    grad_gram = dot_rows(train_gr, val_gr)
    return jnp.sum(in_gram * grad_gram, axis=1)


def local(
    val_inputs, val_out_grad, w_gate, w_up, w_down, val_attn_inputs, train_inputs, train_grads
):
    hid_units = w_gate.shape[1]
    val_count = val_out_grad.shape[0]
    gate_pre = jnp.dot(val_inputs, w_gate, preferred_element_type=jnp.float32)
    up_pre = jnp.dot(val_inputs, w_up, preferred_element_type=jnp.float32)
    hid_grad = dot_rows(val_out_grad, w_down)
    sums = lax.psum_scatter(
        jnp.concatenate([gate_pre, up_pre, hid_grad], axis=1),
        "tok",
        scatter_dimension=0,
        tiled=True,
    )
    grad_gate, grad_up = act_grads(
        sums[:, :hid_units], sums[:, hid_units : 2 * hid_units], sums[:, 2 * hid_units :]
    )
    stacked = jnp.concatenate([grad_gate, grad_up], axis=1)
    piece = lax.all_gather(stacked, "tok", axis=0, tiled=True)
    dx_part = dot_rows(piece[:, :hid_units], w_gate) + dot_rows(piece[:, hid_units:], w_up)
    quarter = val_count // lax.axis_size("hid")
    first_row = lax.axis_index("hid") * quarter
    dx_rows = lax.psum_scatter(dx_part, "hid", scatter_dimension=0, tiled=True)
    own_rows = lax.dynamic_slice_in_dim(val_out_grad, first_row, quarter, 0)
    val_grad = (own_rows.astype(jnp.float32) + dx_rows).astype(jnp.bfloat16)
    attn_full, grad_full = (
        lax.all_gather(val_attn_inputs, "tok", axis=1, tiled=True),
        lax.all_gather(val_grad, "tok", axis=1, tiled=True),
    )
    total = pair_terms(
        train_inputs,
        train_grads,
        lax.all_gather(attn_full, "hid", axis=0, tiled=True),
        lax.all_gather(grad_full, "hid", axis=0, tiled=True),
    )
    influence = total / (train_inputs.shape[1] * math.sqrt(val_count))
    return (influence, val_grad)


def solution(mesh):
    placed = (
        P(None, "tok"),
        P(None, "tok"),
        P("tok", "hid"),
        P("tok", "hid"),
        P("hid", "tok"),
        P("hid", "tok"),
        P(("hid", "tok"), None),
        P(("hid", "tok"), None),
    )
    return jax.shard_map(
        local,
        mesh=mesh,
        in_specs=placed,
        out_specs=(P(("hid", "tok")), P("hid", "tok")),
        check_vma=False,
    )
```

profile of v0, /device:TPU:1, one launch (start us, length us, event | category | flops | bytes accessed | tf_op | source)
XLA Modules:
  0.0 1299.6 jit_solution(1939003087148605138)
XLA Ops:
  7.3 1.8 fusion.13
  9.0 0.7 fusion.14
  9.7 0.7 fusion.15
  10.4 4.4 pad_maximum_fusion
  14.8 0.6 copy-done.7
  15.4 0.6 dynamic-slice
  16.7 697.3 %all-reduce.3.cloned.1.call-done = f32[256,10752]{1,0:T(8,128)} async-done(((f32[256,10752]{1,0:T(8,128)}), f32[256,10752]{1,0:T(8,128)}) %all-reduce.3.cloned.1.call-update) | async-done | bytes 11010064
  713.9 1.1 fusion.11
  715.1 0.6 maximum_bitcast_fusion
  715.8 0.1 copy.14
  715.9 162.7 %all-gather.9.cloned.1.call-done = bf16[64,4,7168]{2,1,0:T(4,128)(2,1)} async-done(((bf16[1,4,7168]{2,1,0:T(4,128)(2,1)}), bf16[64,4,7168]{2,1,0:T(4,128)(2,1)}) %all-gather.9.cloned.1.call-update) | async-done | bytes 3670032 | tf_op jit(solution)/shard_map/all_gather | solution.py:47
  878.6 6.7 reshape.5
  885.3 2.1 fusion
  887.4 2.8 fusion.6
  890.3 155.9 %all_gather.15 = bf16[64,4096]{0,1:T(8,128)(2,1)S(1)} all-gather(bf16[64,64]{0,1:T(8,128)(2,1)S(1)} %copy.14), channel_id=1, replica_groups=mesh['hid'=4,'tok'=64] {'tok'}, dimensions={1}, use_global_device_ids=true | all-gather | bytes 532480 | tf_op jit(solution)/shard_map/all_gather | solution.py:55
  1046.2 1.1 copy.15
  1047.5 0.1 copy.19
  1047.6 0.8 add_convert_fusion
  1048.4 153.2 %all_gather.18 = bf16[64,4096]{0,1:T(8,128)(2,1)S(1)} all-gather(bf16[64,64]{0,1:T(8,128)(2,1)S(1)} %copy.17), channel_id=1, replica_groups=mesh['hid'=4,'tok'=64] {'tok'}, dimensions={1}, use_global_device_ids=true | all-gather | bytes 532480 | tf_op jit(solution)/shard_map/all_gather | solution.py:56
  1201.7 1.1 copy.18
  1202.9 5.0 fusion.12
  1207.9 79.7 %all-gather.7.cloned.1.call-done = bf16[256,4096]{1,0:T(8,128)(2,1)} async-done(((bf16[64,4096]{1,0:T(8,128)(2,1)}), bf16[256,4096]{1,0:T(8,128)(2,1)}) %all-gather.7.cloned.1.call-update) | async-done | bytes 2097168 | tf_op jit(solution)/shard_map/all_gather | solution.py:62
  1287.5 5.0 fusion.5
  1292.5 0.6 broadcast_multiply_fusion
  (29 shorter events, 0.5 us)
Async XLA Ops:
  7.2 1.9 copy-start
  7.2 1.8 copy-start.3
  7.2 2.5 copy-start.1
  7.2 2.5 copy-start.4
  7.2 706.7 %all-reduce.3.cloned.1.call-start = ((), (), s32[]{:S(2)}) async-start(), calls=%async_computation.5 | async-start | bytes 22020096
  14.8 0.7 copy-start.7
  14.8 701.0 %copy-start.6 = (bf16[64,64]{1,0:T(8,128)(2,1)S(1)}, bf16[64,64]{1,0:T(8,128)(2,1)}, u32[]{:S(2)}) copy-start(bf16[64,64]{1,0:T(8,128)(2,1)} %param.13) | copy-start | bytes 24580
  14.8 863.8 %all-gather.9.cloned.1.call-start = ((), (), s32[]{:S(2)}) async-start(), calls=%async_computation.4 | async-start | bytes 3727360 | tf_op jit(solution)/shard_map/all_gather | solution.py:47
  715.7 331.8 %reduce-scatter.2.cloned.1.call-start = ((), (), s32[]{:S(2)}) async-start(), calls=%async_computation.2 | async-start | bytes 163840 | tf_op jit(solution)/shard_map/reduce_scatter | solution.py:51
  715.9 171.5 %copy-start.2 = (bf16[64,3584]{1,0:T(8,128)(2,1)S(1)}, bf16[64,3584]{1,0:T(8,128)(2,1)}, u32[]{:S(2)}) copy-start(bf16[64,3584]{1,0:T(8,128)(2,1)} %param.10) | copy-start | bytes 1376260
  890.2 312.6 %all-gather.5.cloned.1.call-start = ((), (), s32[]{:S(2)}) async-start(), calls=%async_computation.1 | async-start | bytes 2621440 | tf_op jit(solution)/shard_map/all_gather | solution.py:61
  1047.3 240.2 %all-gather.7.cloned.1.call-start = ((), (), s32[]{:S(2)}) async-start(), calls=%async_computation.3 | async-start | bytes 2621440 | tf_op jit(solution)/shard_map/all_gather | solution.py:62
  1048.4 159.5 %copy-start.5 = (bf16[64,64]{1,0:T(8,128)(2,1)}, bf16[64,64]{1,0:T(8,128)(2,1)S(1)}, u32[]{:S(2)}) copy-start(bf16[64,64]{1,0:T(8,128)(2,1)S(1)} %add_convert_fusion) | copy-start | bytes 24580
Sparse Core Ops, SparseCore 0:
  14.9 698.9 all-reduce.2
  717.4 161.1 all-gather.8
  890.4 20.3 reduce-scatter.1
  1047.4 56.4 all-gather.4
  1203.0 84.5 all-gather.6
where the time goes:
time: 1300 us
  waiting for transfers between devices  940 us (72%)
  blocking collectives  309 us (24%)
  matrix products  17.9 us (1%)
  between operations  14.6 us (1%)
    unnamed x6, waiting for transfers between devices  697 us
    all_gather x1, waiting for transfers between devices, local(): piece = lax.all_gather(stacked, 'tok', axis=0, tiled=True)  163 us
    all_gather x1, blocking collectives, local(): lax.all_gather(val_attn_inputs, 'tok', axis=1, tiled=True)  156 us
    all_gather x1, blocking collectives, local(): lax.all_gather(val_grad, 'tok', axis=1, tiled=True)  153 us
    all_gather x1, waiting for transfers between devices, local(): lax.all_gather(grad_full, 'hid', axis=0, tiled=True)  79.7 us
  transfers between devices with their start and end apart: 5, of which 3 were waited for; matrix products, arithmetic and copies ran while one was open for 1% of the time, Pallas kernels for 0%

commit v1 on v0

--- a/solution.py
+++ b/solution.py
@@ -52,7 +52,9 @@
     own_rows = lax.dynamic_slice_in_dim(val_out_grad, first_row, quarter, 0)
     val_grad = (own_rows.astype(jnp.float32) + dx_rows).astype(jnp.bfloat16)
     attn_full, grad_full = (
-        lax.all_gather(val_attn_inputs, "tok", axis=1, tiled=True),
+        jnp.concatenate(
+            lax.all_to_all(jnp.stack([val_attn_inputs] * lax.axis_size("tok")), "tok", 0, 0), axis=1
+        ),
         lax.all_gather(val_grad, "tok", axis=1, tiled=True),
     )
     total = pair_terms(

time: 1300 us -> 1140 us (0.88)
  blocking collectives: 309 us -> 160 us
  waiting for transfers between devices: 940 us -> 915 us
    all_gather x1 -> x0, blocking collectives: 156 us -> none  [local(): lax.all_gather(val_attn_inputs, 'tok', axis=1, tiled=True)]
    all_gather x1, waiting for transfers between devices: 79.7 us -> 46.1 us  [local(): lax.all_gather(grad_full, 'hid', axis=0, tiled=True)]
    reduce_scatter x1, waiting for transfers between devices: 0.02 us -> 17.3 us  [local(): dx_rows = lax.psum_scatter(dx_part, 'hid', scatter_dimension=0, tiled=True)]
  transfers between devices with their start and end apart: 5 -> 6, of which waited for: 3 -> 4; matrix products, arithmetic and copies ran while one was open for 1% -> 2% of each run, Pallas kernels for 0% -> 0%
where the time goes in v1:
time: 1140 us
  waiting for transfers between devices  915 us (80%)
  blocking collectives  160 us (14%)
  matrix products  17.9 us (2%)
  between operations  14.6 us (1%)
  local copies, waits for them, and re-layouts  14.1 us (1%)
    unnamed x6, waiting for transfers between devices  697 us
    all_gather x1, blocking collectives, local(): lax.all_gather(val_grad, 'tok', axis=1, tiled=True)  160 us
    all_gather x1, waiting for transfers between devices, local(): piece = lax.all_gather(stacked, 'tok', axis=0, tiled=True)  155 us
    all_gather x1, waiting for transfers between devices, local(): lax.all_gather(grad_full, 'hid', axis=0, tiled=True)  46.1 us
  transfers between devices with their start and end apart: 6, of which 4 were waited for; matrix products, arithmetic and copies ran while one was open for 2% of the time, Pallas kernels for 0%

profile of v1, /device:TPU:1, one launch (start us, length us, event | category | flops | bytes accessed | tf_op | source)
XLA Modules:
  0.0 1137.2 jit_solution(18255794344701324148)
XLA Ops:
  7.3 1.8 fusion.13
  9.0 0.7 fusion.14
  9.7 0.7 fusion.15
  10.4 4.4 pad_maximum_fusion
  14.8 0.6 copy-done.7
  16.7 697.3 %all-reduce.3.cloned.1.call-done = f32[256,10752]{1,0:T(8,128)} async-done(((f32[256,10752]{1,0:T(8,128)}), f32[256,10752]{1,0:T(8,128)}) %all-reduce.3.cloned.1.call-update) | async-done | bytes 11010064
  713.9 1.1 fusion.11
  715.1 0.6 maximum_bitcast_fusion
  716.0 1.5 reshape.17
  717.5 7.7 all-to-all-start
  725.4 154.7 %all-gather.9.cloned.1.call-done = bf16[64,4,7168]{2,1,0:T(4,128)(2,1)} async-done(((bf16[1,4,7168]{2,1,0:T(4,128)(2,1)}), bf16[64,4,7168]{2,1,0:T(4,128)(2,1)}) %all-gather.9.cloned.1.call-update) | async-done | bytes 3670032 | tf_op jit(solution)/shard_map/all_gather | solution.py:47
  880.0 6.7 reshape.15
  886.7 2.1 fusion
  888.9 2.8 fusion.6
  891.7 0.7 reshape.18
  892.4 0.7 copy.15
  893.1 1.6 reshape.13
  895.0 17.3 %reduce-scatter.2.cloned.1.call-done = f32[64,64]{1,0:T(8,128)} async-done(((f32[256,64]{1,0:T(8,128)}), f32[64,64]{1,0:T(8,128)}) %reduce-scatter.2.cloned.1.call-update) | async-done | bytes 16400 | tf_op jit(solution)/shard_map/reduce_scatter | solution.py:51
  912.2 0.8 add_convert_fusion
  913.1 159.8 %all_gather.14 = bf16[64,4096]{0,1:T(8,128)(2,1)S(1)} all-gather(bf16[64,64]{0,1:T(8,128)(2,1)S(1)} %copy.17), channel_id=1, replica_groups=mesh['hid'=4,'tok'=64] {'tok'}, dimensions={1}, use_global_device_ids=true | all-gather | bytes 532480 | tf_op jit(solution)/shard_map/all_gather | solution.py:58
  1072.9 1.1 copy.18
  1074.1 5.0 fusion.12
  1079.1 46.1 %all-gather.7.cloned.1.call-done = bf16[256,4096]{1,0:T(8,128)(2,1)} async-done(((bf16[64,4096]{1,0:T(8,128)(2,1)}), bf16[256,4096]{1,0:T(8,128)(2,1)}) %all-gather.7.cloned.1.call-update) | async-done | bytes 2097168 | tf_op jit(solution)/shard_map/all_gather | solution.py:64
  1125.1 5.0 fusion.5
  (33 shorter events, 2.0 us)
Async XLA Ops:
  7.2 1.9 copy-start
  7.2 1.8 copy-start.3
  7.2 2.5 copy-start.1
  7.2 2.5 copy-start.4
  7.2 706.7 %all-reduce.3.cloned.1.call-start = ((), (), s32[]{:S(2)}) async-start(), calls=%async_computation.6 | async-start | bytes 22020096
  14.7 0.7 copy-start.7
  14.8 701.0 %copy-start.6 = (bf16[64,64]{1,0:T(8,128)(2,1)S(1)}, bf16[64,64]{1,0:T(8,128)(2,1)}, u32[]{:S(2)}) copy-start(bf16[64,64]{1,0:T(8,128)(2,1)} %param.13) | copy-start | bytes 24580
  14.8 865.2 %all-gather.9.cloned.1.call-start = ((), (), s32[]{:S(2)}) async-start(), calls=%async_computation.5 | async-start | bytes 3727360 | tf_op jit(solution)/shard_map/all_gather | solution.py:47
  717.5 174.2 %all-to-all-start = ((bf16[64,2,2048]{2,1,0:T(2,128)(2,1)}), bf16[64,2,2048]{2,1,0:T(2,128)(2,1)S(1)}, u32[]{:S(2)}, u32[]{:S(2)}) async-start(bf16[64,2,2048]{2,1,0:T(2,128)(2,1)} %reshape.17), calls=%async_computation | async-start | bytes 1048576 | tf_op jit(solution)/shard_map/all_to_all | solution.py:56
  725.3 163.6 %copy-start.2 = (bf16[64,3584]{1,0:T(8,128)(2,1)S(1)}, bf16[64,3584]{1,0:T(8,128)(2,1)}, u32[]{:S(2)}) copy-start(bf16[64,3584]{1,0:T(8,128)(2,1)} %param.10) | copy-start | bytes 1376260
  725.3 186.9 %reduce-scatter.2.cloned.1.call-start = ((), (), s32[]{:S(2)}) async-start(), calls=%async_computation.3 | async-start | bytes 163840 | tf_op jit(solution)/shard_map/reduce_scatter | solution.py:51
  891.7 182.4 %all-gather.5.cloned.1.call-start = ((), (), s32[]{:S(2)}) async-start(), calls=%async_computation.2 | async-start | bytes 2621440 | tf_op jit(solution)/shard_map/all_gather | solution.py:63
  894.7 230.4 %all-gather.7.cloned.1.call-start = ((), (), s32[]{:S(2)}) async-start(), calls=%async_computation.4 | async-start | bytes 2621440 | tf_op jit(solution)/shard_map/all_gather | solution.py:64
  913.0 166.1 %copy-start.5 = (bf16[64,64]{1,0:T(8,128)(2,1)}, bf16[64,64]{1,0:T(8,128)(2,1)S(1)}, u32[]{:S(2)}) copy-start(bf16[64,64]{1,0:T(8,128)(2,1)S(1)} %add_convert_fusion) | copy-start | bytes 24580
Sparse Core Ops, SparseCore 0:
  14.9 698.9 all-reduce.2
  717.4 162.5 all-gather.8
  891.8 20.3 reduce-scatter.1
  913.9 32.7 all-gather.4
  1074.2 50.9 all-gather.6
